TPU v7x, 128 devices: a whole 4x4x4 slice. The times are simulated.
128 devices in a mesh: row: 16 (over x, y), col: 4 (over z), layer: 2 (over core).
Axes of the slice: x: 4, y: 4, z: 4, core: 2. Of those that a mesh axis runs over, the one named last changes fastest.
Arguments:
- density: float32 [4096, 4096], P('row', ('col', 'layer')), may hold values from -2 to 2
- masks: int32 [6, 64, 64], replicated, may hold values from 0 to 1, as said below
- branch: int32 [5], replicated, may hold values from 0 to 1, as said below
- perm: int32 [64], replicated, may hold values from 0 to 63, each once
Outputs:
- purified: float32 [4096, 4096], P('row', ('col', 'layer'))
Inputs may be any that keep to these rules, and one draw needn't show every extreme that they name: masks are symmetric in their last two dimensions, every diagonal block is occupied, and block (i, j) of masks[s] is occupied only where the cyclic distance between i and j is at most 6 + s. `branch`: both values occur among the steps. `perm`: a permutation of 0..63.
All inputs are finite; a program needn't handle non-finite values.
Results may differ from a plain program's by a relative error of at most 0.0003.
Values sent between devices are 32-bit elements; how exact they have to be, the bound alone decides.
No kernel may reach another device: no remote copies, remote signals or barrier semaphores. Data moves between devices by JAX's collectives and lax.ppermute only.
A program may use at most 64 MiB of HBM per device.

v0:
```python
import jax
import jax.numpy as jnp
from jax import lax
from jax.sharding import PartitionSpec as P

BS = 64
STEPS = 5


def expand(block_mask):
    grown = jnp.repeat(block_mask, BS, axis=0)
    return jnp.repeat(grown, BS, axis=1).astype(jnp.float32)


def shards(density, masks, branch, perm):
    rows_here = density.shape[0]
    cols_here = density.shape[1]
    row_blocks = rows_here // BS
    col_blocks = cols_here // BS
    row_start = lax.axis_index("row") * row_blocks
    col_start = lax.axis_index(("col", "layer")) * col_blocks
    row_ids = lax.dynamic_slice_in_dim(perm, row_start, row_blocks)
    col_ids = lax.dynamic_slice_in_dim(perm, col_start, col_blocks)
    local_masks = jnp.take(jnp.take(masks, row_ids, axis=1), col_ids, axis=2)
    current = density * expand(local_masks[0])
    for step in range(STEPS):
        panel = lax.all_gather(current, ("col", "layer"), axis=1, tiled=True)
        square = jnp.dot(
            panel,
            lax.all_gather(current, "row", axis=0, tiled=True),
            preferred_element_type=jnp.float32,
            precision=lax.Precision.HIGHEST,
        )
        picked = jnp.where(branch[step] == 1, 2.0 * current - square, square)
        current = picked * expand(local_masks[step + 1])
    return current


def solution(mesh):
    return jax.shard_map(
        shards,
        mesh=mesh,
        in_specs=(P("row", ("col", "layer")), P(), P(), P()),
        out_specs=P("row", ("col", "layer")),
        check_vma=False,
    )
```

profile of v0, /device:TPU:1, one launch (start us, length us, event | category | flops | bytes accessed | tf_op | source)
XLA Modules:
  0.0 603.6 jit_solution(2125554987655784131)
XLA Ops:
  6.5 0.8 compare_and_fusion
  7.5 0.6 gather_fusion
  8.3 0.7 compare_and_fusion.1
  9.0 0.6 gather_fusion.1
  10.2 1.9 mul.45
  12.2 0.7 all-gather.13.cloned.1.call-update
  13.5 1.5 fusion.11
  15.5 32.8 %all-gather.11.cloned.1.call-done = f32[256,4096]{1,0:T(8,128)} async-done(((f32[256,512]{1,0:T(8,128)}), f32[256,4096]{1,0:T(8,128)}) %all-gather.11.cloned.1.call-update) | async-done | bytes 4194320 | tf_op jit(solution)/shard_map/all_gather | solution.py:27
  48.3 72.2 %all-gather.13.cloned.1.call-done = f32[4096,512]{1,0:T(8,128)} async-done(((f32[256,512]{1,0:T(8,128)}), f32[4096,512]{1,0:T(8,128)}) %all-gather.13.cloned.1.call-update) | async-done | bytes 8388624 | tf_op jit(solution)/shard_map/all_gather | solution.py:30
  120.5 11.5 %fusion = f32[256,512]{1,0:T(8,128)} fusion(f32[256,512]{1,0:T(8,128)S(1)} %copy.29, f32[256,512]{1,0:T(8,128)} %mul.45, pred[]{:T(512)} %bitcast.4, f32[256,4096]{1,0:T(8,128)} %all-gather.11.cloned.1.call-done, f32[4096,512]{1,0:T(8,128)} %all-gather.13.cloned.1.call-done), kind=kOutput, calls=%fused_computation.7 | convolution fusion | flops 6442975232 | bytes 14155777 | tf_op jit(solution)/shard_map/dot_general | solution.py:28
  132.0 0.5 all-gather.17.cloned.1.call-update
  133.8 30.8 %all-gather.15.cloned.1.call-done = f32[256,4096]{1,0:T(8,128)} async-done(((f32[256,512]{1,0:T(8,128)}), f32[256,4096]{1,0:T(8,128)}) %all-gather.15.cloned.1.call-update) | async-done | bytes 4194320 | tf_op jit(solution)/shard_map/all_gather | solution.py:27
  164.6 72.0 %all-gather.17.cloned.1.call-done = f32[4096,512]{1,0:T(8,128)} async-done(((f32[256,512]{1,0:T(8,128)}), f32[4096,512]{1,0:T(8,128)}) %all-gather.17.cloned.1.call-update) | async-done | bytes 8388624 | tf_op jit(solution)/shard_map/all_gather | solution.py:30
  236.6 11.5 %fusion.1 = f32[256,512]{1,0:T(8,128)} fusion(f32[256,512]{1,0:T(8,128)S(1)} %copy.31, f32[256,512]{1,0:T(8,128)} %fusion, pred[]{:T(512)} %bitcast.3, f32[256,4096]{1,0:T(8,128)} %all-gather.15.cloned.1.call-done, f32[4096,512]{1,0:T(8,128)} %all-gather.17.cloned.1.call-done), kind=kOutput, calls=%fused_computation.8 | convolution fusion | flops 6442975232 | bytes 14155777 | tf_op jit(solution)/shard_map/dot_general | solution.py:28
  250.1 30.7 %all-gather.19.cloned.1.call-done = f32[256,4096]{1,0:T(8,128)} async-done(((f32[256,512]{1,0:T(8,128)}), f32[256,4096]{1,0:T(8,128)}) %all-gather.19.cloned.1.call-update) | async-done | bytes 4194320 | tf_op jit(solution)/shard_map/all_gather | solution.py:27
  280.8 72.0 %all-gather.21.cloned.1.call-done = f32[4096,512]{1,0:T(8,128)} async-done(((f32[256,512]{1,0:T(8,128)}), f32[4096,512]{1,0:T(8,128)}) %all-gather.21.cloned.1.call-update) | async-done | bytes 8388624 | tf_op jit(solution)/shard_map/all_gather | solution.py:30
  352.8 11.5 %fusion.2 = f32[256,512]{1,0:T(8,128)} fusion(f32[256,512]{1,0:T(8,128)S(1)} %copy.33, f32[256,512]{1,0:T(8,128)} %fusion.1, pred[]{:T(512)} %bitcast.2, f32[256,4096]{1,0:T(8,128)} %all-gather.19.cloned.1.call-done, f32[4096,512]{1,0:T(8,128)} %all-gather.21.cloned.1.call-done), kind=kOutput, calls=%fused_computation.9 | convolution fusion | flops 6442975232 | bytes 14155777 | tf_op jit(solution)/shard_map/dot_general | solution.py:28
  364.4 0.7 all-gather.25.cloned.1.call-update
  366.2 30.7 %all-gather.23.cloned.1.call-done = f32[256,4096]{1,0:T(8,128)} async-done(((f32[256,512]{1,0:T(8,128)}), f32[256,4096]{1,0:T(8,128)}) %all-gather.23.cloned.1.call-update) | async-done | bytes 4194320 | tf_op jit(solution)/shard_map/all_gather | solution.py:27
  397.0 72.2 %all-gather.25.cloned.1.call-done = f32[4096,512]{1,0:T(8,128)} async-done(((f32[256,512]{1,0:T(8,128)}), f32[4096,512]{1,0:T(8,128)}) %all-gather.25.cloned.1.call-update) | async-done | bytes 8388624 | tf_op jit(solution)/shard_map/all_gather | solution.py:30
  469.1 11.5 %fusion.3 = f32[256,512]{1,0:T(8,128)} fusion(f32[256,512]{1,0:T(8,128)S(1)} %copy.35, f32[256,512]{1,0:T(8,128)} %fusion.2, pred[]{:T(512)} %bitcast.1, f32[256,4096]{1,0:T(8,128)} %all-gather.23.cloned.1.call-done, f32[4096,512]{1,0:T(8,128)} %all-gather.25.cloned.1.call-done), kind=kOutput, calls=%fused_computation.10 | convolution fusion | flops 6442975232 | bytes 14155777 | tf_op jit(solution)/shard_map/dot_general | solution.py:28
  482.4 30.8 %all-gather.27.cloned.1.call-done = f32[256,4096]{1,0:T(8,128)} async-done(((f32[256,512]{1,0:T(8,128)}), f32[256,4096]{1,0:T(8,128)}) %all-gather.27.cloned.1.call-update) | async-done | bytes 4194320 | tf_op jit(solution)/shard_map/all_gather | solution.py:27
  513.2 72.0 %all-gather.29.cloned.1.call-done = f32[4096,512]{1,0:T(8,128)} async-done(((f32[256,512]{1,0:T(8,128)}), f32[4096,512]{1,0:T(8,128)}) %all-gather.29.cloned.1.call-update) | async-done | bytes 8388624 | tf_op jit(solution)/shard_map/all_gather | solution.py:30
  585.3 11.5 %fusion.4 = f32[256,512]{1,0:T(8,128)} fusion(f32[256,512]{1,0:T(8,128)S(1)} %copy.37, f32[256,512]{1,0:T(8,128)} %fusion.3, pred[]{:T(512)} %bitcast, f32[256,4096]{1,0:T(8,128)} %all-gather.27.cloned.1.call-done, f32[4096,512]{1,0:T(8,128)} %all-gather.29.cloned.1.call-done), kind=kOutput, calls=%fused_computation.11 | convolution fusion | flops 6442975232 | bytes 14155777 | tf_op jit(solution)/shard_map/dot_general | solution.py:28
  (58 shorter events, 5.1 us)
Async XLA Ops:
  6.5 0.9 copy-start
  6.5 41.8 %all-gather.11.cloned.1.call-start = ((), (), s32[]{:S(2)}) async-start(), calls=%async_computation | async-start | bytes 4718592 | tf_op jit(solution)/shard_map/all_gather | solution.py:27
  12.2 108.3 %all-gather.13.cloned.1.call-start = ((), (), s32[]{:S(2)}) async-start(), calls=%async_computation.1 | async-start | bytes 8912896 | tf_op jit(solution)/shard_map/all_gather | solution.py:30
  12.9 151.7 %all-gather.15.cloned.1.call-start = ((), (), s32[]{:S(2)}) async-start(), calls=%async_computation.2 | async-start | bytes 4718592 | tf_op jit(solution)/shard_map/all_gather | solution.py:27
  132.0 104.7 %all-gather.17.cloned.1.call-start = ((), (), s32[]{:S(2)}) async-start(), calls=%async_computation.3 | async-start | bytes 8912896 | tf_op jit(solution)/shard_map/all_gather | solution.py:30
  132.6 148.2 %all-gather.19.cloned.1.call-start = ((), (), s32[]{:S(2)}) async-start(), calls=%async_computation.4 | async-start | bytes 4718592 | tf_op jit(solution)/shard_map/all_gather | solution.py:27
  248.1 104.7 %all-gather.21.cloned.1.call-start = ((), (), s32[]{:S(2)}) async-start(), calls=%async_computation.5 | async-start | bytes 8912896 | tf_op jit(solution)/shard_map/all_gather | solution.py:30
  248.7 148.3 %all-gather.23.cloned.1.call-start = ((), (), s32[]{:S(2)}) async-start(), calls=%async_computation.6 | async-start | bytes 4718592 | tf_op jit(solution)/shard_map/all_gather | solution.py:27
  364.3 104.8 %all-gather.25.cloned.1.call-start = ((), (), s32[]{:S(2)}) async-start(), calls=%async_computation.7 | async-start | bytes 8912896 | tf_op jit(solution)/shard_map/all_gather | solution.py:30
  365.1 148.2 %all-gather.27.cloned.1.call-start = ((), (), s32[]{:S(2)}) async-start(), calls=%async_computation.8 | async-start | bytes 4718592 | tf_op jit(solution)/shard_map/all_gather | solution.py:27
  480.6 116.1 %copy-start.1 = (s32[6,64,64]{2,1,0:T(8,128)S(1)}, s32[6,64,64]{2,1,0:T(8,128)}, u32[]{:S(2)}) copy-start(s32[6,64,64]{2,1,0:T(8,128)} %param.5) | copy-start | bytes 294916
  480.6 104.6 %all-gather.29.cloned.1.call-start = ((), (), s32[]{:S(2)}) async-start(), calls=%async_computation.9 | async-start | bytes 8912896 | tf_op jit(solution)/shard_map/all_gather | solution.py:30
Sparse Core Ops, SparseCore 0:
  12.3 35.9 all-gather.10
  50.5 69.9 all-gather.12
  132.1 32.4 all-gather.14
  166.6 69.9 all-gather.16
  248.3 32.5 all-gather.18
  282.8 69.9 all-gather.20
  364.4 32.4 all-gather.22
  399.1 69.9 all-gather.24
  480.7 32.4 all-gather.26
  515.2 69.9 all-gather.28
where the time goes:
time: 604 us
  waiting for transfers between devices  519 us (86%)
  matrix products  57.3 us (9%)
  between operations  16.9 us (3%)
    all_gather x5, waiting for transfers between devices, shards(): lax.all_gather(current, 'row', axis=0, tiled=True)  360 us
    all_gather x5, waiting for transfers between devices, shards(): panel = lax.all_gather(current, ('col', 'layer'), axis=1, tiled=True)  156 us
    dot_general x5, matrix products, shards(): jnp.dot(panel, lax.all_gather(current, 'row', axis=0, tiled=True), prefer...  57.3 us
  transfers between devices with their start and end apart: 10, of which 10 were waited for; matrix products, arithmetic and copies ran while one was open for 1% of the time, Pallas kernels for 0%

commit v1 on v0

--- a/solution.py
+++ b/solution.py
@@ -5,6 +5,14 @@
 
 BS = 64
 STEPS = 5
+
+
+def gather_by_exchange(shard, axis, dim):
+    peers = lax.axis_size(axis)
+    repeats = [peers if d == dim else 1 for d in range(shard.ndim)]
+    return lax.all_to_all(
+        jnp.tile(shard, repeats), axis, split_axis=dim, concat_axis=dim, tiled=True
+    )
 
 
 def expand(block_mask):
@@ -27,7 +35,7 @@
         panel = lax.all_gather(current, ("col", "layer"), axis=1, tiled=True)
         square = jnp.dot(
             panel,
-            lax.all_gather(current, "row", axis=0, tiled=True),
+            gather_by_exchange(current, "row", 0),
             preferred_element_type=jnp.float32,
             precision=lax.Precision.HIGHEST,
         )

time: 604 us -> 745 us (1.23)
  the two profiles are of different devices: /device:TPU:1 before, /device:TPU:124 now
where the time goes in v1:
time: 745 us; the launch traced here: 744 us
  waiting for transfers between devices  607 us (81%)
  matrix products  55.6 us (7%)
  starting transfers between devices  35.6 us (5%)
  local copies, waits for them, and re-layouts  26.8 us (4%)
  between operations  16.6 us (2%)
    all_to_all x5, waiting for transfers between devices, gather_by_exchange(): lax.all_to_all(jnp.tile(shard, repeats), axis, split_axis=dim, concat_axi...  445 us
    all_gather x5, waiting for transfers between devices, shards(): panel = lax.all_gather(current, ('col', 'layer'), axis=1, tiled=True)  159 us
    dot_general x5, matrix products, shards(): jnp.dot(panel, gather_by_exchange(current, 'row', 0), preferred_element_t...  55.6 us
    all_to_all x5, starting transfers between devices, gather_by_exchange(): lax.all_to_all(jnp.tile(shard, repeats), axis, split_axis=dim, concat_axi...  35 us
    another operation x5, local copies, waits for them, and re-layouts, gather_by_exchange(): jnp.tile(shard, repeats)  21.7 us
  transfers between devices with their start and end apart: 10, of which 10 were waited for; matrix products, arithmetic and copies ran while one was open for 0% of the time, Pallas kernels for 0%

profile of v1, /device:TPU:124, one launch (start us, length us, event | category | flops | bytes accessed | tf_op | source)
XLA Modules:
  0.0 743.9 jit_solution(14752514617441286529)
XLA Ops:
  11.4 4.3 tile.10
  15.7 7.2 all-to-all-start
  25.5 31.3 %all-gather.6.cloned.1.call-done = f32[256,4096]{1,0:T(8,128)} async-done(((f32[256,512]{1,0:T(8,128)}), f32[256,4096]{1,0:T(8,128)}) %all-gather.6.cloned.1.call-update) | async-done | bytes 4194320 | tf_op jit(solution)/shard_map/all_gather | solution.py:35
  56.7 115.3 %all-to-all-done = f32[16,256,512]{2,1,0:T(8,128)} async-done(((f32[16,256,512]{2,1,0:T(8,128)}), f32[16,256,512]{2,1,0:T(8,128)}, u32[]{:S(2)}, u32[]{:S(2)}) %all-to-all-start) | async-done | bytes 8388640 | tf_op jit(solution)/shard_map/all_to_all | solution.py:13
  172.1 11.0 %fusion = f32[256,512]{1,0:T(8,128)S(1)} fusion(f32[256,512]{1,0:T(8,128)S(1)} %copy.29, f32[256,512]{1,0:T(8,128)} %copy-done.3, pred[]{:T(512)} %bitcast.4, f32[256,4096]{1,0:T(8,128)} %all-gather.6.cloned.1.call-done, f32[4096,512]{1,0:T(8,128)} %bitcast.9), kind=kOutput, calls=%fused_computation.7 | convolution fusion | flops 6442975232 | bytes 14155777 | tf_op jit(solution)/shard_map/dot_general | solution.py:36
  183.1 4.3 tile.11
  187.5 6.9 all-to-all-start.1
  196.3 31.9 %all-gather.8.cloned.1.call-done = f32[256,4096]{1,0:T(8,128)} async-done(((f32[256,512]{1,0:T(8,128)}), f32[256,4096]{1,0:T(8,128)}) %all-gather.8.cloned.1.call-update) | async-done | bytes 4194320 | tf_op jit(solution)/shard_map/all_gather | solution.py:35
  228.2 100.5 %all-to-all-done.1 = f32[16,256,512]{2,1,0:T(8,128)} async-done(((f32[16,256,512]{2,1,0:T(8,128)}), f32[16,256,512]{2,1,0:T(8,128)}, u32[]{:S(2)}, u32[]{:S(2)}) %all-to-all-start.1) | async-done | bytes 8388640 | tf_op jit(solution)/shard_map/all_to_all | solution.py:13
  328.7 11.0 %fusion.1 = f32[256,512]{1,0:T(8,128)S(1)} fusion(f32[256,512]{1,0:T(8,128)S(1)} %copy.31, f32[256,512]{1,0:T(8,128)} %copy-done.4, pred[]{:T(512)} %bitcast.3, f32[256,4096]{1,0:T(8,128)} %all-gather.8.cloned.1.call-done, f32[4096,512]{1,0:T(8,128)} %bitcast.12), kind=kOutput, calls=%fused_computation.8 | convolution fusion | flops 6442975232 | bytes 14155777 | tf_op jit(solution)/shard_map/dot_general | solution.py:36
  339.7 4.3 tile.12
  344.1 6.9 all-to-all-start.2
  352.9 31.9 %all-gather.10.cloned.1.call-done = f32[256,4096]{1,0:T(8,128)} async-done(((f32[256,512]{1,0:T(8,128)}), f32[256,4096]{1,0:T(8,128)}) %all-gather.10.cloned.1.call-update) | async-done | bytes 4194320 | tf_op jit(solution)/shard_map/all_gather | solution.py:35
  384.8 86.8 %all-to-all-done.2 = f32[16,256,512]{2,1,0:T(8,128)} async-done(((f32[16,256,512]{2,1,0:T(8,128)}), f32[16,256,512]{2,1,0:T(8,128)}, u32[]{:S(2)}, u32[]{:S(2)}) %all-to-all-start.2) | async-done | bytes 8388640 | tf_op jit(solution)/shard_map/all_to_all | solution.py:13
  471.6 11.0 %fusion.2 = f32[256,512]{1,0:T(8,128)S(1)} fusion(f32[256,512]{1,0:T(8,128)S(1)} %copy.33, f32[256,512]{1,0:T(8,128)} %copy-done.5, pred[]{:T(512)} %bitcast.2, f32[256,4096]{1,0:T(8,128)} %all-gather.10.cloned.1.call-done, f32[4096,512]{1,0:T(8,128)} %bitcast.15), kind=kOutput, calls=%fused_computation.9 | convolution fusion | flops 6442975232 | bytes 14155777 | tf_op jit(solution)/shard_map/dot_general | solution.py:36
  487.0 6.9 all-to-all-start.3
  495.7 31.8 %all-gather.12.cloned.1.call-done = f32[256,4096]{1,0:T(8,128)} async-done(((f32[256,512]{1,0:T(8,128)}), f32[256,4096]{1,0:T(8,128)}) %all-gather.12.cloned.1.call-update) | async-done | bytes 4194320 | tf_op jit(solution)/shard_map/all_gather | solution.py:35
  527.5 64.7 %all-to-all-done.3 = f32[16,256,512]{2,1,0:T(8,128)} async-done(((f32[16,256,512]{2,1,0:T(8,128)}), f32[16,256,512]{2,1,0:T(8,128)}, u32[]{:S(2)}, u32[]{:S(2)}) %all-to-all-start.3) | async-done | bytes 8388640 | tf_op jit(solution)/shard_map/all_to_all | solution.py:13
  592.1 11.0 %fusion.3 = f32[256,512]{1,0:T(8,128)S(1)} fusion(f32[256,512]{1,0:T(8,128)S(1)} %copy.35, f32[256,512]{1,0:T(8,128)} %copy-done.6, pred[]{:T(512)} %bitcast.1, f32[256,4096]{1,0:T(8,128)} %all-gather.12.cloned.1.call-done, f32[4096,512]{1,0:T(8,128)} %bitcast.18), kind=kOutput, calls=%fused_computation.10 | convolution fusion | flops 6442975232 | bytes 14155777 | tf_op jit(solution)/shard_map/dot_general | solution.py:36
  603.2 4.3 tile.14
  607.5 6.9 all-to-all-start.4
  616.2 31.8 %all-gather.14.cloned.1.call-done = f32[256,4096]{1,0:T(8,128)} async-done(((f32[256,512]{1,0:T(8,128)}), f32[256,4096]{1,0:T(8,128)}) %all-gather.14.cloned.1.call-update) | async-done | bytes 4194320 | tf_op jit(solution)/shard_map/all_gather | solution.py:35
  647.9 78.0 %all-to-all-done.4 = f32[16,256,512]{2,1,0:T(8,128)} async-done(((f32[16,256,512]{2,1,0:T(8,128)}), f32[16,256,512]{2,1,0:T(8,128)}, u32[]{:S(2)}, u32[]{:S(2)}) %all-to-all-start.4) | async-done | bytes 8388640 | tf_op jit(solution)/shard_map/all_to_all | solution.py:13
  725.9 11.5 %fusion.4 = f32[256,512]{1,0:T(8,128)} fusion(f32[256,512]{1,0:T(8,128)S(1)} %copy.37, f32[256,512]{1,0:T(8,128)} %copy-done.2, pred[]{:T(512)} %bitcast, f32[256,4096]{1,0:T(8,128)} %all-gather.14.cloned.1.call-done, f32[4096,512]{1,0:T(8,128)} %bitcast.21), kind=kOutput, calls=%fused_computation.11 | convolution fusion | flops 6442975232 | bytes 14155777 | tf_op jit(solution)/shard_map/dot_general | solution.py:36
  (70 shorter events, 15.5 us)
Async XLA Ops:
  6.5 0.9 copy-start
  11.3 4.4 copy-start.3
  15.7 8.5 %copy-start.7 = (s32[5]{0:T(128)S(1)}, s32[5]{0:T(128)}, u32[]{:S(2)}) copy-start(s32[5]{0:T(128)} %param.6) | copy-start | bytes 64
  15.7 156.4 %all-to-all-start = ((f32[16,256,512]{2,1,0:T(8,128)}), f32[16,256,512]{2,1,0:T(8,128)}, u32[]{:S(2)}, u32[]{:S(2)}) async-start(f32[16,256,512]{2,1,0:T(8,128)} %tile.10), calls=%async_computation | async-start | bytes 16777216 | tf_op jit(solution)/shard_map/all_to_all | solution.py:13
  22.9 33.8 %all-gather.6.cloned.1.call-start = ((), (), s32[]{:S(2)}) async-start(), calls=%async_computation.5 | async-start | bytes 4718592 | tf_op jit(solution)/shard_map/all_gather | solution.py:35
  183.1 4.4 copy-start.4
  187.5 141.2 %all-to-all-start.1 = ((f32[16,256,512]{2,1,0:T(8,128)}), f32[16,256,512]{2,1,0:T(8,128)}, u32[]{:S(2)}, u32[]{:S(2)}) async-start(f32[16,256,512]{2,1,0:T(8,128)} %tile.11), calls=%async_computation.1 | async-start | bytes 16777216 | tf_op jit(solution)/shard_map/all_to_all | solution.py:13
  194.4 33.8 %all-gather.8.cloned.1.call-start = ((), (), s32[]{:S(2)}) async-start(), calls=%async_computation.6 | async-start | bytes 4718592 | tf_op jit(solution)/shard_map/all_gather | solution.py:35
  339.7 4.4 copy-start.5
  344.1 127.6 %all-to-all-start.2 = ((f32[16,256,512]{2,1,0:T(8,128)}), f32[16,256,512]{2,1,0:T(8,128)}, u32[]{:S(2)}, u32[]{:S(2)}) async-start(f32[16,256,512]{2,1,0:T(8,128)} %tile.12), calls=%async_computation.2 | async-start | bytes 16777216 | tf_op jit(solution)/shard_map/all_to_all | solution.py:13
  351.0 33.8 %all-gather.10.cloned.1.call-start = ((), (), s32[]{:S(2)}) async-start(), calls=%async_computation.7 | async-start | bytes 4718592 | tf_op jit(solution)/shard_map/all_gather | solution.py:35
  482.7 4.4 copy-start.6
  487.0 105.1 %all-to-all-start.3 = ((f32[16,256,512]{2,1,0:T(8,128)}), f32[16,256,512]{2,1,0:T(8,128)}, u32[]{:S(2)}, u32[]{:S(2)}) async-start(f32[16,256,512]{2,1,0:T(8,128)} %tile.13), calls=%async_computation.3 | async-start | bytes 16777216 | tf_op jit(solution)/shard_map/all_to_all | solution.py:13
  494.0 33.5 %all-gather.12.cloned.1.call-start = ((), (), s32[]{:S(2)}) async-start(), calls=%async_computation.8 | async-start | bytes 4718592 | tf_op jit(solution)/shard_map/all_gather | solution.py:35
  603.2 4.4 copy-start.2
  607.5 118.4 %all-to-all-start.4 = ((f32[16,256,512]{2,1,0:T(8,128)}), f32[16,256,512]{2,1,0:T(8,128)}, u32[]{:S(2)}, u32[]{:S(2)}) async-start(f32[16,256,512]{2,1,0:T(8,128)} %tile.14), calls=%async_computation.4 | async-start | bytes 16777216 | tf_op jit(solution)/shard_map/all_to_all | solution.py:13
  614.4 122.9 %copy-start.1 = (s32[6,64,64]{2,1,0:T(8,128)S(1)}, s32[6,64,64]{2,1,0:T(8,128)}, u32[]{:S(2)}) copy-start(s32[6,64,64]{2,1,0:T(8,128)} %param.5) | copy-start | bytes 294916
  614.4 33.5 %all-gather.14.cloned.1.call-start = ((), (), s32[]{:S(2)}) async-start(), calls=%async_computation.9 | async-start | bytes 4718592 | tf_op jit(solution)/shard_map/all_gather | solution.py:35
Sparse Core Ops, SparseCore 0:
  25.5 31.2 all-gather.5
  196.9 31.2 all-gather.7
  353.5 31.2 all-gather.9
  496.2 31.2 all-gather.11
  616.7 31.2 all-gather.13
